TPU v7x, 128 devices: a whole 4x4x4 slice. The times are simulated.
128 devices in a mesh: dp: 32 (over x, z, core), enc: 4 (over y).
Axes of the slice: x: 4, y: 4, z: 4, core: 2. Of those that a mesh axis runs over, the one named last changes fastest.
Arguments:
- hidden: bfloat16 [16384, 4096], P('dp', 'enc'), may hold values from -6 to 6
- norm_gain: float32 [4096], replicated, may hold values from 0.25 to 1.75
- w_query: bfloat16 [4096, 2048], P('dp', 'enc'), may hold values from -0.09375 to 0.09375
- w_key: bfloat16 [896, 2048], P('dp', 'enc'), may hold values from -0.1875 to 0.1875
- w_value: bfloat16 [896, 2048], P('dp', 'enc'), may hold values from -0.1875 to 0.1875
- w_out: bfloat16 [2048, 4096], P('enc', 'dp'), may hold values from -0.125 to 0.125
- w_cond: bfloat16 [4096, 896], P('dp', 'enc'), may hold values from -0.75 to 0.75
- enc_gain: float32 [896], replicated, may hold values from 0.25 to 1.75
- store: bfloat16 [1024, 128, 896], P(('dp', 'enc')), may hold values from -6 to 6
- neighbour_ids: int32 [512], P(('dp', 'enc')), may hold values from 0 to 1023, as said below
- out_grad: bfloat16 [16384, 4096], P('dp', 'enc'), may hold values from -6 to 6
Outputs:
- layer_out: bfloat16 [16384, 4096], P('dp', 'enc')
- hidden_grad: float32 [16384, 4096], P('dp', 'enc')
- query_grad: float32 [4096, 2048], P('dp', 'enc')
- key_grad: float32 [896, 2048], P('dp', 'enc')
- value_grad: float32 [896, 2048], P('dp', 'enc')
- out_weight_grad: float32 [2048, 4096], P('enc', 'dp')
- cond_grad: float32 [4096, 896], P('dp', 'enc')
Inputs may be any that keep to these rules, and one draw needn't show every extreme that they name: `neighbour_ids`: slot n names a neighbour stored on a device of the same data index as the device holding slot n (device k holds rows k * 8 to (k + 1) * 8 - 1). Among the 4 slots of one device at most 2 name rows of one device, and for every data index one device is named by exactly 2 slots of each of the 4 devices.
All inputs are finite; a program needn't handle non-finite values.
Results may differ from a plain program's by a relative error of at most 0.019.
Values may be sent and summed in bfloat16 or wider, within the bound.
A program may use at most 192 MiB of HBM per device.

v0:
```python
import jax
import jax.numpy as jnp
from jax import lax
from jax.sharding import PartitionSpec as P

HSZ = 128
SPAN = 64
NBR = 2
NL = 128
epsilon = 1e-05


def side_by_side(arrays, axis, dim, along):
    ends, at = ([], 0)
    for a in arrays[:-1]:
        at += a.shape[along]
        ends.append(at)
    both = jnp.concatenate(arrays, axis=along)
    return tuple(jnp.split(lax.all_gather(both, axis, axis=dim, tiled=True), ends, axis=along))


def joined_along(tiles, dim):
    tiles = jnp.moveaxis(tiles, 0, dim)
    dims = tiles.shape
    return tiles.reshape(*dims[:dim], dims[dim] * dims[dim + 1], *dims[dim + 2 :])


def copy_for_each(shard, axis):
    copies = jnp.broadcast_to(shard, (lax.axis_size(axis), *shard.shape))
    return lax.all_to_all(copies, axis, split_axis=0, concat_axis=0, tiled=True)


def collect(shard, axis, dim):
    return joined_along(copy_for_each(shard, axis), dim)


def in_blocks(shard, dim, peers):
    dims = shard.shape
    tiles = shard.reshape(*dims[:dim], peers, dims[dim] // peers, *dims[dim + 1 :])
    return jnp.moveaxis(tiles, dim, 0)


def summed_on_arrival(shard, axis, dim):
    peers = lax.axis_size(axis)
    tiles = lax.all_to_all(in_blocks(shard, dim, peers), axis, 0, 0, tiled=True)
    return jnp.sum(tiles.astype(jnp.float32), axis=0)


def one_scatter(arrays, axis, dims):
    peers = lax.axis_size(axis)
    tiles = [in_blocks(a, dim, peers) for a, dim in zip(arrays, dims)]
    lines = jnp.concatenate([b.reshape(peers, -1) for b in tiles], axis=1)
    extent = max(16, -(-lines.shape[1] // 1024) * 8)
    lines = jnp.pad(lines, ((0, 0), (0, extent * 128 - lines.shape[1]))).reshape(-1, 128)
    flat, at, done = (lax.psum_scatter(lines, axis, tiled=True).reshape(-1), 0, [])
    for b in tiles:
        part = b[0]
        done.append(flat[at : at + part.size].reshape(part.shape))
        at += part.size
    return tuple(done)


def rms_scale(values):
    return lax.rsqrt(jnp.mean(values * values, axis=-1, keepdims=True) + epsilon)


def encoder_input(raw_rows, cond_rows):
    enc_in = raw_rows.astype(jnp.float32) + cond_rows.astype(jnp.float32)[..., None, :]
    return (enc_in, rms_scale(enc_in))


def encode_rows(raw_rows, cond_rows, enc_gain):
    enc_in, enc_rstd = encoder_input(raw_rows, cond_rows)
    return (enc_in * enc_rstd * enc_gain).astype(jnp.bfloat16)


def cond_gradient(raw_rows, cond_rows, enc_gain, grad_rows):
    enc_in, enc_rstd = encoder_input(raw_rows, cond_rows)
    scaled_enc = enc_gain * grad_rows.astype(jnp.float32)
    enc_mean = jnp.mean(enc_in * scaled_enc, axis=-1, keepdims=True)
    return jnp.sum(enc_rstd * scaled_enc - enc_in * enc_rstd**3 * enc_mean, axis=-2)


def contract_first(left, right):
    return lax.dot_general(
        left, right, (((0,), (0,)), ((), ())), preferred_element_type=jnp.float32
    )


def contract_last(left, right):
    return lax.dot_general(
        left, right, (((1,), (1,)), ((), ())), preferred_element_type=jnp.float32
    )


def shards(
    hidden,
    norm_gain,
    w_query,
    w_key,
    w_value,
    w_out,
    w_cond,
    enc_gain,
    store,
    neighbour_ids,
    out_grad,
):
    groups = lax.axis_size("enc")
    member = lax.axis_index("enc")
    tok_rows = hidden.shape[0]
    feature_cols = hidden.shape[1]
    model_width = feature_cols * groups
    head_cols = w_query.shape[1]
    enc_width = w_key.shape[0] * lax.axis_size("dp")
    enc_cols = w_cond.shape[1]
    span_count = tok_rows // SPAN
    requests = neighbour_ids.shape[0]
    capacity = max(2, (requests + 1) // 2)
    store_rows = store.shape[0]
    heads_here = head_cols // HSZ
    keys_len = NBR * NL
    score_scale = HSZ ** (-0.5)
    full_rows = lax.all_gather(hidden, "enc", axis=1, tiled=True)
    inputs = full_rows.astype(jnp.float32)
    row_rstd = rms_scale(inputs)
    normed = (inputs * row_rstd * norm_gain).astype(jnp.bfloat16)
    w_query_all, w_key_all, w_value_all, w_cond_all = (
        lax.all_gather(w_query, "dp", axis=0, tiled=True),
        *side_by_side((w_key, w_value), "dp", 0, 1),
        lax.all_gather(w_cond, "dp", axis=0, tiled=True),
    )
    queries = jnp.dot(normed, w_query_all, preferred_element_type=jnp.float32).astype(jnp.bfloat16)
    w_out_all = lax.all_gather(w_out, "dp", axis=1, tiled=True)
    summary = jnp.mean(inputs.reshape(span_count, SPAN, model_width), axis=1).astype(jnp.bfloat16)
    cond_part = jnp.dot(summary, w_cond_all, preferred_element_type=jnp.float32).astype(
        jnp.bfloat16
    )
    condition = collect(cond_part, "enc", 1)
    request_order = jnp.arange(requests)
    my_spans = (member * requests + request_order) // NBR
    cond_req = jnp.take(condition, my_spans, axis=0)
    owner_of = neighbour_ids // store_rows % groups
    store_row = neighbour_ids % store_rows
    earlier = (owner_of[:, None] == owner_of[None, :]) & (
        request_order[None, :] < request_order[:, None]
    )
    slot_rank = jnp.sum(earlier.astype(jnp.int32), axis=1)
    slot_index = owner_of * capacity + slot_rank
    selection = slot_index[None, :] == jnp.arange(groups * capacity)[:, None]
    row_buffer = jnp.sum(jnp.where(selection, store_row[None, :], 0), axis=1).reshape(
        groups, capacity
    )
    raw_buffer = lax.all_to_all(
        jnp.take(
            store,
            lax.all_to_all(row_buffer, "enc", split_axis=0, concat_axis=0, tiled=True),
            axis=0,
        ),
        "enc",
        split_axis=0,
        concat_axis=0,
        tiled=True,
    )
    raw_mine = jnp.take(raw_buffer.reshape(groups * capacity, NL, enc_width), slot_index, axis=0)
    encoded_mine = encode_rows(raw_mine, cond_req, enc_gain)
    encoded = lax.all_gather(encoded_mine, "enc", axis=0, tiled=True)
    flat_enc = encoded.reshape(-1, enc_width)
    keys_proj = jnp.dot(flat_enc, w_key_all, preferred_element_type=jnp.float32).astype(
        jnp.bfloat16
    )
    values_proj = jnp.dot(flat_enc, w_value_all, preferred_element_type=jnp.float32).astype(
        jnp.bfloat16
    )
    query_heads = queries.reshape(span_count, SPAN, heads_here, HSZ)
    key_heads = keys_proj.reshape(span_count, keys_len, heads_here, HSZ)
    value_heads = values_proj.reshape(span_count, keys_len, heads_here, HSZ)
    scores = (
        jnp.einsum("cqhd,ckhd->chqk", query_heads, key_heads, preferred_element_type=jnp.float32)
        * score_scale
    )
    attn_full = jax.nn.softmax(scores, axis=-1)
    attn_weights = attn_full.astype(jnp.bfloat16)
    attended = (
        jnp.einsum("chqk,ckhd->cqhd", attn_weights, value_heads, preferred_element_type=jnp.float32)
        .astype(jnp.bfloat16)
        .reshape(tok_rows, head_cols)
    )
    out_term = jnp.dot(attended, w_out_all, preferred_element_type=jnp.float32)
    projected = summed_on_arrival(out_term.astype(jnp.bfloat16), "enc", 1)
    layer_out = (hidden.astype(jnp.float32) + projected).astype(jnp.bfloat16)
    grad_rows = lax.all_gather(out_grad, "enc", axis=1, tiled=True)
    attended_grad = contract_last(grad_rows, w_out_all).astype(jnp.bfloat16)
    out_weight_grad = lax.psum_scatter(
        contract_first(attended, grad_rows).astype(jnp.bfloat16),
        "dp",
        scatter_dimension=1,
        tiled=True,
    ).astype(jnp.float32)
    grad_heads = attended_grad.reshape(span_count, SPAN, heads_here, HSZ)
    prob_grad = jnp.einsum(
        "cqhd,ckhd->chqk", grad_heads, value_heads, preferred_element_type=jnp.float32
    )
    score_grad = (
        attn_full
        * (prob_grad - jnp.sum(attn_full * prob_grad, axis=-1, keepdims=True))
        * score_scale
    ).astype(jnp.bfloat16)
    query_act_grad = (
        jnp.einsum("chqk,ckhd->cqhd", score_grad, key_heads, preferred_element_type=jnp.float32)
        .astype(jnp.bfloat16)
        .reshape(tok_rows, head_cols)
    )
    key_act_grad = (
        jnp.einsum("chqk,cqhd->ckhd", score_grad, query_heads, preferred_element_type=jnp.float32)
        .astype(jnp.bfloat16)
        .reshape(-1, head_cols)
    )
    value_act_grad = (
        jnp.einsum("chqk,cqhd->ckhd", attn_weights, grad_heads, preferred_element_type=jnp.float32)
        .astype(jnp.bfloat16)
        .reshape(-1, head_cols)
    )
    query_grad = lax.psum_scatter(
        contract_first(normed, query_act_grad).astype(jnp.bfloat16),
        "dp",
        scatter_dimension=0,
        tiled=True,
    ).astype(jnp.float32)
    enc_term = contract_last(key_act_grad, w_key_all) + contract_last(value_act_grad, w_value_all)
    encoded_grad = (
        summed_on_arrival(enc_term.astype(jnp.bfloat16), "enc", 0)
        .astype(jnp.bfloat16)
        .reshape(requests, NL, enc_width)
    )
    cond_mine = cond_gradient(raw_mine, cond_req, enc_gain, encoded_grad)
    slot_grads = collect(cond_mine, "enc", 0)
    cond_delta = jnp.sum(slot_grads.reshape(span_count, NBR, enc_width), axis=1).astype(
        jnp.bfloat16
    )
    delta_cols = lax.dynamic_slice_in_dim(cond_delta, member * enc_cols, enc_cols, 1)
    key_term = contract_first(flat_enc, key_act_grad)
    value_term = contract_first(flat_enc, value_act_grad)
    cond_term = contract_first(summary, delta_cols)
    key_grad, value_grad, cond_grad = tuple(
        (
            part.astype(jnp.float32)
            for part in one_scatter(
                (
                    key_term.astype(jnp.bfloat16),
                    value_term.astype(jnp.bfloat16),
                    cond_term.astype(jnp.bfloat16),
                ),
                "dp",
                (0, 0, 0),
            )
        )
    )
    summary_term = contract_last(delta_cols, w_cond_all)
    normed_term = contract_last(query_act_grad, w_query_all)
    normed_grad, summary_grad = (
        lax.psum(normed_term.astype(jnp.bfloat16), "enc").astype(jnp.float32),
        lax.psum(summary_term.astype(jnp.bfloat16), "enc").astype(jnp.float32),
    )
    scaled = normed_grad * norm_gain
    row_mean = jnp.mean(inputs * scaled, axis=-1, keepdims=True)
    full_grad = (
        grad_rows.astype(jnp.float32)
        + (row_rstd * scaled - inputs * row_rstd**3 * row_mean)
        + jnp.repeat(summary_grad / SPAN, SPAN, axis=0)
    )
    hidden_grad = lax.dynamic_slice_in_dim(full_grad, member * feature_cols, feature_cols, 1)
    return (layer_out, hidden_grad, query_grad, key_grad, value_grad, out_weight_grad, cond_grad)


def solution(mesh):
    placed = (
        P("dp", "enc"),
        P(),
        P("dp", "enc"),
        P("dp", "enc"),
        P("dp", "enc"),
        P("enc", "dp"),
        P("dp", "enc"),
        P(),
        P(("dp", "enc"), None, None),
        P(("dp", "enc")),
        P("dp", "enc"),
    )
    return jax.shard_map(
        shards,
        mesh=mesh,
        in_specs=placed,
        out_specs=(
            P("dp", "enc"),
            P("dp", "enc"),
            P("dp", "enc"),
            P("dp", "enc"),
            P("dp", "enc"),
            P("enc", "dp"),
            P("dp", "enc"),
        ),
        check_vma=False,
    )
```

profile of v0, /device:TPU:0, one launch (start us, length us, event | category | flops | bytes accessed | tf_op | source)
XLA Modules:
  0.0 741.9 jit_solution(10964547584921568469)
XLA Ops:
  11.8 9.6 %all_to_all.40 = s32[4,1,2]{2,1,0:T(1,128)S(1)} all-to-all(s32[4,1,2]{2,1,0:T(1,128)S(1)} %bitcast.99), channel_id=1, replica_groups=mesh['dp'=32,'enc'=4] {'enc'}, dimensions={0} | all-to-all | bytes 64 | tf_op jit(solution)/shard_map/all_to_all | solution.py:157
  30.6 49.5 %all-gather.9.cloned.1.call-done = bf16[512,4096]{1,0:T(8,128)(2,1)} async-done(((bf16[512,1024]{1,0:T(8,128)(2,1)}), bf16[512,4096]{1,0:T(8,128)(2,1)}) %all-gather.9.cloned.1.call-update) | async-done | bytes 4194320 | tf_op jit(solution)/shard_map/all_gather | solution.py:124
  83.1 43.9 %all-gather.11.cloned.1.call-done = bf16[4096,224]{0,1:T(8,128)(2,1)} async-done(((bf16[128,224]{0,1:T(8,128)(2,1)}), bf16[4096,224]{0,1:T(8,128)(2,1)}) %all-gather.11.cloned.1.call-update) | async-done | bytes 1835024 | tf_op jit(solution)/shard_map/all_gather | solution.py:131
  144.0 29.2 %all-gather.21.cloned.1.call-done = bf16[32,28,1024]{2,1,0:T(8,128)(2,1)} async-done(((bf16[1,28,1024]{2,1,0:T(8,128)(2,1)}), bf16[32,28,1024]{2,1,0:T(8,128)(2,1)}) %all-gather.21.cloned.1.call-update) | async-done | bytes 1835024 | tf_op jit(solution)/shard_map/all_gather | solution.py:19
  180.6 40.4 %all-gather.15.cloned.1.call-done = bf16[4096,512]{1,0:T(8,128)(2,1)} async-done(((bf16[128,512]{1,0:T(8,128)(2,1)}), bf16[4096,512]{1,0:T(8,128)(2,1)}) %all-gather.15.cloned.1.call-update) | async-done | bytes 4194320 | tf_op jit(solution)/shard_map/all_gather | solution.py:129
  221.0 5.8 convolution_convert_fusion.11
  227.0 39.4 %all-gather.13.cloned.1.call-done = bf16[16,128,896]{2,1,0:T(8,128)(2,1)} async-done(((bf16[4,128,896]{2,1,0:T(8,128)(2,1)}), bf16[16,128,896]{2,1,0:T(8,128)(2,1)}) %all-gather.13.cloned.1.call-update) | async-done | bytes 3670032 | tf_op jit(solution)/shard_map/all_gather | solution.py:167
  266.4 5.9 convolution_convert_fusion.6
  276.3 6.4 convolution_convert_fusion.7
  291.4 6.0 fusion.34
  297.7 18.7 %all-gather.19.cloned.1.call-done = bf16[512,4096]{1,0:T(8,128)(2,1)} async-done(((bf16[512,1024]{1,0:T(8,128)(2,1)}), bf16[512,4096]{1,0:T(8,128)(2,1)}) %all-gather.19.cloned.1.call-update) | async-done | bytes 4194320 | tf_op jit(solution)/shard_map/all_gather | solution.py:192
  316.4 6.5 convolution_convert_fusion
  323.0 6.5 copy.112
  329.9 38.4 %all-gather.17.cloned.1.call-done = bf16[512,4096]{1,0:T(8,128)(2,1)} async-done(((bf16[512,128]{1,0:T(8,128)(2,1)}), bf16[512,4096]{1,0:T(8,128)(2,1)}) %all-gather.17.cloned.1.call-update) | async-done | bytes 4194320 | tf_op jit(solution)/shard_map/all_gather | solution.py:134
  378.1 16.3 %fusion.37 = bf16[8,64,4,128]{3,1,2,0:T(8,128)(2,1)} fusion(bf16[8,256,4,128]{3,2,1,0:T(4,128)(2,1)} %reshape.289, f32[8,4,64,256]{3,2,1,0:T(8,128)} %fusion.9, f32[8,4,64,256]{3,2,1,0:T(8,128)} %get-tuple-element.50, f32[8,4,64]{2,1,0:T(4,128)S(1)} %get-tuple-element.49), kind=kOutput, calls=%fused_computation.62 | convolution fusion | flops 138152192 | bytes 6823936 | tf_op jit(solution)/shard_map/chqk,ckhd->cqhd/dot_general | solution.py:210
  395.9 6.8 convolution_convert_fusion.1
  402.7 16.7 %convert_bitcast_fusion.1 = bf16[8,256,4,128]{1,3,2,0:T(8,128)(2,1)} fusion(f32[8,4,64,256]{3,2,1,0:T(8,128)} %fusion.9, bf16[8,64,4,128]{3,2,1,0:T(4,128)(2,1)S(1)} %reshape.288, f32[8,4,64,256]{3,2,1,0:T(8,128)} %get-tuple-element.50, f32[8,4,64]{2,1,0:T(4,128)S(1)} %get-tuple-element.49), kind=kOutput, calls=%fused_computation.29 | convolution fusion | flops 138938624 | bytes 6823936 | tf_op jit(solution)/shard_map/chqk,cqhd->ckhd/dot_general | solution.py:215
  424.4 7.0 convert_bitcast_fusion
  448.9 6.7 convolution_convert_fusion.2
  461.8 31.0 %all-to-all-done.4 = bf16[4,512,896]{2,1,0:T(8,128)(2,1)} async-done(((bf16[4,512,896]{2,1,0:T(8,128)(2,1)}), bf16[4,512,896]{2,1,0:T(8,128)(2,1)}, u32[]{:S(2)}, u32[]{:S(2)}) %all-to-all-start.4) | async-done | bytes 3670048 | tf_op jit(solution)/shard_map/all_to_all | solution.py:45
  536.3 6.5 convert_element_type.163
  542.8 36.6 %all-to-all-done.3 = bf16[4,512,1024]{2,1,0:T(8,128)(2,1)} async-done(((bf16[4,512,1024]{2,1,0:T(8,128)(2,1)}), bf16[4,512,1024]{2,1,0:T(8,128)(2,1)}, u32[]{:S(2)}, u32[]{:S(2)}) %all-to-all-start.3) | async-done | bytes 4194336 | tf_op jit(solution)/shard_map/all_to_all | solution.py:45
  587.7 58.2 %all-reduce.3.cloned.1.call-done = (bf16[8,4096]{1,0:T(8,128)(2,1)}, bf16[512,4096]{1,0:T(8,128)(2,1)}) async-done(((bf16[8,4096]{1,0:T(8,128)(2,1)}, bf16[512,4096]{1,0:T(8,128)(2,1)}), (bf16[8,4096]{1,0:T(8,128)(2,1)}, bf16[512,4096]{1,0:T(8,128)(2,1)})) %all-reduce.3.cloned.1.call-update) | async-done | bytes 4259856 | tf_op jit(solution)/shard_map/psum | solution.py:263
  655.9 75.2 %reduce-scatter.8.cloned.1.call-done = bf16[448,128]{1,0:T(8,128)(2,1)} async-done(((bf16[14336,128]{1,0:T(8,128)(2,1)}), bf16[448,128]{1,0:T(8,128)(2,1)}) %reduce-scatter.8.cloned.1.call-update) | async-done | bytes 114704 | tf_op jit(solution)/shard_map/reduce_scatter | solution.py:55
  (169 shorter events, 159.6 us)
Async XLA Ops:
  7.2 72.9 %all-gather.9.cloned.1.call-start = ((), (), s32[]{:S(2)}) async-start(), calls=%async_computation.9 | async-start | bytes 5242880 | tf_op jit(solution)/shard_map/all_gather | solution.py:124
  7.9 119.2 %all-gather.11.cloned.1.call-start = ((), (), s32[]{:S(2)}) async-start(), calls=%async_computation.10 | async-start | bytes 1892352 | tf_op jit(solution)/shard_map/all_gather | solution.py:131
  8.7 164.6 %all-gather.21.cloned.1.call-start = ((), (), s32[]{:S(2)}) async-start(), calls=%async_computation.17 | async-start | bytes 2162688 | tf_op jit(solution)/shard_map/all_gather | solution.py:19
  10.2 210.9 %all-gather.15.cloned.1.call-start = ((), (), s32[]{:S(2)}) async-start(), calls=%async_computation.12 | async-start | bytes 4325376 | tf_op jit(solution)/shard_map/all_gather | solution.py:129
  11.6 129.7 %copy-start.19 = (pred[4]{0:T(512)(128)(4,1)}, pred[4]{0:T(512)(128)(4,1)S(1)}, u32[]{:S(2)}) copy-start(pred[4]{0:T(512)(128)(4,1)S(1)} %get-tuple-element.37) | copy-start | bytes 16
  26.9 102.2 %all-to-all-start.1 = ((bf16[4,2,128,896]{3,2,1,0:T(8,128)(2,1)}), bf16[4,2,128,896]{3,2,1,0:T(8,128)(2,1)S(1)}, u32[]{:S(2)}, u32[]{:S(2)}) async-start(bf16[4,2,128,896]{3,2,1,0:T(8,128)(2,1)} %broadcast_select_fusion), calls=%async_computation.1 | async-start | bytes 3670016 | tf_op jit(solution)/shard_map/all_to_all | solution.py:154
  83.1 58.1 %copy-start.13 = (f32[896]{0:T(1024)S(1)}, f32[896]{0:T(1024)}, u32[]{:S(2)}) copy-start(f32[896]{0:T(1024)} %param.18) | copy-start | bytes 10756
  129.8 9.7 %all-to-all-start.2 = ((bf16[4,8,224]{2,1,0:T(8,128)(2,1)}), bf16[4,8,224]{2,1,0:T(8,128)(2,1)S(1)}, u32[]{:S(2)}, u32[]{:S(2)}) async-start(bf16[4,8,224]{2,1,0:T(8,128)(2,1)} %broadcast_in_dim.82), calls=%async_computation.2 | async-start | bytes 32768 | tf_op jit(solution)/shard_map/all_to_all | solution.py:30
  134.1 132.3 %all-gather.13.cloned.1.call-start = ((), (), s32[]{:S(2)}) async-start(), calls=%async_computation.11 | async-start | bytes 4587520 | tf_op jit(solution)/shard_map/all_gather | solution.py:167
  141.3 35.7 %copy-start.15 = (f32[4,128]{1,0:T(4,128)}, f32[4,128]{1,0:T(4,128)S(1)}, u32[]{:S(2)}) copy-start(f32[4,128]{1,0:T(4,128)S(1)} %get-tuple-element.46) | copy-start | bytes 6148
  142.6 173.8 %all-gather.19.cloned.1.call-start = ((), (), s32[]{:S(2)}) async-start(), calls=%async_computation.14 | async-start | bytes 5242880 | tf_op jit(solution)/shard_map/all_gather | solution.py:192
  143.2 225.1 %all-gather.17.cloned.1.call-start = ((), (), s32[]{:S(2)}) async-start(), calls=%async_computation.13 | async-start | bytes 4325376 | tf_op jit(solution)/shard_map/all_gather | solution.py:134
  144.0 440.3 %reduce-scatter.10.cloned.1.call-start = ((), (), s32[]{:S(2)}) async-start(), calls=%async_computation.18 | async-start | bytes 4325376
  177.0 44.1 %copy-start.17 = (f32[4096]{0:T(1024)S(1)}, f32[4096]{0:T(1024)}, u32[]{:S(2)}) copy-start(f32[4096]{0:T(1024)} %param.12) | copy-start | bytes 49156
  180.6 215.2 %copy-start.22 = (f32[512]{0:T(512)}, f32[512]{0:T(512)S(1)}, u32[]{:S(2)}) copy-start(f32[512]{0:T(512)S(1)} %get-tuple-element.44) | copy-start | bytes 6148
  329.5 256.6 %reduce-scatter.6.cloned.1.call-start = ((), (), s32[]{:S(2)}) async-start(), calls=%async_computation.15 | async-start | bytes 4325376 | tf_op jit(solution)/shard_map/reduce_scatter | solution.py:224
  443.9 48.9 %all-to-all-start.4 = ((bf16[4,512,896]{2,1,0:T(8,128)(2,1)}), bf16[4,512,896]{2,1,0:T(8,128)(2,1)}, u32[]{:S(2)}, u32[]{:S(2)}) async-start(bf16[4,512,896]{2,1,0:T(8,128)(2,1)} %bitcast.88), calls=%async_computation.4 | async-start | bytes 7340032 | tf_op jit(solution)/shard_map/all_to_all | solution.py:45
  497.9 13.9 %all-to-all-start.5 = ((f32[4,4,896]{2,1,0:T(4,128)}), f32[4,4,896]{2,1,0:T(4,128)S(1)}, u32[]{:S(2)}, u32[]{:S(2)}) async-start(f32[4,4,896]{2,1,0:T(4,128)} %broadcast_in_dim.84), calls=%async_computation.5 | async-start | bytes 114688 | tf_op jit(solution)/shard_map/all_to_all | solution.py:30
  511.8 67.6 %all-to-all-start.3 = ((bf16[4,512,1024]{2,1,0:T(8,128)(2,1)}), bf16[4,512,1024]{2,1,0:T(8,128)(2,1)}, u32[]{:S(2)}, u32[]{:S(2)}) async-start(bf16[4,512,1024]{2,1,0:T(8,128)(2,1)} %bitcast.80), calls=%async_computation.3 | async-start | bytes 8388608 | tf_op jit(solution)/shard_map/all_to_all | solution.py:45
  516.7 129.2 %all-reduce.3.cloned.1.call-start = ((), (), s32[]{:S(2)}) async-start(), calls=%async_computation.19 | async-start | bytes 8519680 | tf_op jit(solution)/shard_map/psum | solution.py:263
  527.7 203.4 %reduce-scatter.8.cloned.1.call-start = ((), (), s32[]{:S(2)}) async-start(), calls=%async_computation.16 | async-start | bytes 3784704 | tf_op jit(solution)/shard_map/reduce_scatter | solution.py:55
  542.8 40.1 %copy-start.3 = (bf16[512,1024]{1,0:T(8,128)(2,1)S(1)}, bf16[512,1024]{1,0:T(8,128)(2,1)}, u32[]{:S(2)}) copy-start(bf16[512,1024]{1,0:T(8,128)(2,1)} %param.11) | copy-start | bytes 3145732
  582.9 63.0 %copy-start.18 = (f32[4096]{0:T(1024)S(1)}, f32[4096]{0:T(1024)}, u32[]{:S(2)}) copy-start(f32[4096]{0:T(1024)} %param.12) | copy-start | bytes 49156
  651.9 83.0 %copy-start.1 = (bf16[8,128,896]{2,1,0:T(8,128)(2,1)S(1)}, bf16[8,128,896]{2,1,0:T(8,128)(2,1)}, u32[]{:S(2)}) copy-start(bf16[8,128,896]{2,1,0:T(8,128)(2,1)} %param.19) | copy-start | bytes 5505028
  (18 other events, 195.6 us)
Sparse Core Ops, SparseCore 0:
  9.7 70.3 all-gather.8
  82.3 44.7 all-gather.10
  129.9 43.2 all-gather.20
  175.4 45.6 all-gather.14
  223.1 43.2 all-gather.12
  267.9 48.4 all-gather.18
  318.6 49.7 all-gather.16
  372.0 81.5 reduce-scatter.9
  457.7 81.2 reduce-scatter.5
  541.9 103.9 all-reduce.2
  650.0 81.0 reduce-scatter.7
where the time goes:
time: 752 us; the launch traced here: 742 us
  waiting for transfers between devices  467 us (62%)
  matrix products  119 us (16%)
  local copies, waits for them, and re-layouts  60.3 us (8%)
  other arithmetic  48.4 us (6%)
  starting transfers between devices  22.4 us (3%)
  between operations  14.9 us (2%)
  blocking collectives  9.59 us (1%)
    reduce_scatter x1, waiting for transfers between devices, one_scatter(): lax.psum_scatter(lines, axis, tiled=True).reshape(-1)  75.2 us
    all_to_all x2, waiting for transfers between devices, summed_on_arrival(): tiles = lax.all_to_all(in_blocks(shard, dim, peers), axis, 0, 0, tiled=True)  67.6 us
    psum x1, waiting for transfers between devices, shards(): lax.psum(summary_term.astype(jnp.bfloat16), 'enc').astype(jnp.float32)  58.2 us
    all_gather x1, waiting for transfers between devices, shards(): full_rows = lax.all_gather(hidden, 'enc', axis=1, tiled=True)  49.5 us
    all_gather x1, waiting for transfers between devices, shards(): lax.all_gather(w_cond, 'dp', axis=0, tiled=True)  43.9 us
    all_gather x1, waiting for transfers between devices, shards(): lax.all_gather(w_query, 'dp', axis=0, tiled=True)  40.4 us
    all_gather x1, waiting for transfers between devices, shards(): encoded = lax.all_gather(encoded_mine, 'enc', axis=0, tiled=True)  39.4 us
    all_gather x1, waiting for transfers between devices, shards(): w_out_all = lax.all_gather(w_out, 'dp', axis=1, tiled=True)  38.4 us
  transfers between devices with their start and end apart: 16, of which 12 were waited for; matrix products, arithmetic and copies ran while one was open for 30% of the time, Pallas kernels for 0%

commit v1 on v0

--- a/solution.py
+++ b/solution.py
@@ -2,12 +2,14 @@
 import jax.numpy as jnp
 from jax import lax
 from jax.sharding import PartitionSpec as P
+from jax.lax import all_gather
 
 HSZ = 128
 SPAN = 64
 NBR = 2
 NL = 128
 epsilon = 1e-05
+pass_the_routes_all = lambda q_in, group_axis: all_gather(q_in, group_axis).sum(axis=0)
 
 
 def side_by_side(arrays, axis, dim, along):
@@ -260,7 +262,7 @@
     normed_term = contract_last(query_act_grad, w_query_all)
     normed_grad, summary_grad = (
         lax.psum(normed_term.astype(jnp.bfloat16), "enc").astype(jnp.float32),
-        lax.psum(summary_term.astype(jnp.bfloat16), "enc").astype(jnp.float32),
+        pass_the_routes_all(summary_term.astype(jnp.bfloat16), "enc").astype(jnp.float32),
     )
     scaled = normed_grad * norm_gain
     row_mean = jnp.mean(inputs * scaled, axis=-1, keepdims=True)

time: 752 us -> 816 us (1.085)
  blocking collectives: 9.59 us -> 57.7 us
  waiting for transfers between devices: 467 us -> 490 us
    psum x1, waiting for transfers between devices: 58.2 us -> 0.01 us  [shards(): lax.psum(normed_term.astype(jnp.bfloat16), 'enc').astype(jnp.float32)]
    all_gather x0 -> x1, blocking collectives: none -> 48.1 us  [all_gather(q_in, group_axis).sum(axis=0)]
    reduce_scatter x1, waiting for transfers between devices: 0.01 us -> 47.3 us  [shards(): lax.psum_scatter(contract_first(normed, query_act_grad).astype(jnp.bfloat...]
    all_gather x1, waiting for transfers between devices: 18.7 us -> 43.1 us  [shards(): grad_rows = lax.all_gather(out_grad, 'enc', axis=1, tiled=True)]
    all_to_all x2, waiting for transfers between devices: 67.6 us -> 54.1 us  [summed_on_arrival(): tiles = lax.all_to_all(in_blocks(shard, dim, peers), axis, 0, 0, tiled=True)]
    all_gather x1, waiting for transfers between devices: 38.4 us -> 51.8 us  [shards(): w_out_all = lax.all_gather(w_out, 'dp', axis=1, tiled=True)]
    unnamed x58 -> x44, local copies, waits for them, and re-layouts: 17.1 us -> 18.5 us
  transfers between devices with their start and end apart: 16 -> 16, of which waited for: 12 -> 11; matrix products, arithmetic and copies ran while one was open for 30% -> 21% of each run, Pallas kernels for 0% -> 0%
where the time goes in v1:
time: 816 us; the launch traced here: 810 us
  waiting for transfers between devices  490 us (60%)
  matrix products  116 us (14%)
  local copies, waits for them, and re-layouts  62.9 us (8%)
  blocking collectives  57.7 us (7%)
  other arithmetic  47.1 us (6%)
  starting transfers between devices  21.9 us (3%)
  between operations  14.5 us (2%)
    reduce_scatter x1, waiting for transfers between devices, one_scatter(): lax.psum_scatter(lines, axis, tiled=True).reshape(-1)  83 us
    all_to_all x2, waiting for transfers between devices, summed_on_arrival(): tiles = lax.all_to_all(in_blocks(shard, dim, peers), axis, 0, 0, tiled=True)  54.1 us
    all_gather x1, waiting for transfers between devices, shards(): w_out_all = lax.all_gather(w_out, 'dp', axis=1, tiled=True)  51.8 us
    all_gather x1, waiting for transfers between devices, shards(): full_rows = lax.all_gather(hidden, 'enc', axis=1, tiled=True)  49.1 us
    all_gather x1, blocking collectives, all_gather(q_in, group_axis).sum(axis=0)  48.1 us
    reduce_scatter x1, waiting for transfers between devices, shards(): lax.psum_scatter(contract_first(normed, query_act_grad).astype(jnp.bfloat...  47.3 us
    all_gather x1, waiting for transfers between devices, shards(): lax.all_gather(w_cond, 'dp', axis=0, tiled=True)  43.9 us
    all_gather x1, waiting for transfers between devices, shards(): grad_rows = lax.all_gather(out_grad, 'enc', axis=1, tiled=True)  43.1 us
  transfers between devices with their start and end apart: 16, of which 11 were waited for; matrix products, arithmetic and copies ran while one was open for 21% of the time, Pallas kernels for 0%

profile of v1, /device:TPU:0, one launch (start us, length us, event | category | flops | bytes accessed | tf_op | source)
XLA Modules:
  0.0 810.5 jit_solution(6479084069623310542)
XLA Ops:
  12.3 9.6 %all_to_all.40 = s32[4,1,2]{2,1,0:T(1,128)S(1)} all-to-all(s32[4,1,2]{2,1,0:T(1,128)S(1)} %bitcast.101), channel_id=1, replica_groups=mesh['dp'=32,'enc'=4] {'enc'}, dimensions={0} | all-to-all | bytes 64 | tf_op jit(solution)/shard_map/all_to_all | solution.py:159
  31.0 49.1 %all-gather.10.cloned.1.call-done = bf16[512,4096]{1,0:T(8,128)(2,1)} async-done(((bf16[512,1024]{1,0:T(8,128)(2,1)}), bf16[512,4096]{1,0:T(8,128)(2,1)}) %all-gather.10.cloned.1.call-update) | async-done | bytes 4194320 | tf_op jit(solution)/shard_map/all_gather | solution.py:126
  83.2 43.9 %all-gather.12.cloned.1.call-done = bf16[4096,224]{0,1:T(8,128)(2,1)} async-done(((bf16[128,224]{0,1:T(8,128)(2,1)}), bf16[4096,224]{0,1:T(8,128)(2,1)}) %all-gather.12.cloned.1.call-update) | async-done | bytes 1835024 | tf_op jit(solution)/shard_map/all_gather | solution.py:133
  142.4 30.8 %all-gather.22.cloned.1.call-done = bf16[32,28,1024]{2,1,0:T(8,128)(2,1)} async-done(((bf16[1,28,1024]{2,1,0:T(8,128)(2,1)}), bf16[32,28,1024]{2,1,0:T(8,128)(2,1)}) %all-gather.22.cloned.1.call-update) | async-done | bytes 1835024 | tf_op jit(solution)/shard_map/all_gather | solution.py:21
  180.1 41.0 %all-gather.16.cloned.1.call-done = bf16[4096,512]{1,0:T(8,128)(2,1)} async-done(((bf16[128,512]{1,0:T(8,128)(2,1)}), bf16[4096,512]{1,0:T(8,128)(2,1)}) %all-gather.16.cloned.1.call-update) | async-done | bytes 4194320 | tf_op jit(solution)/shard_map/all_gather | solution.py:131
  221.1 5.8 convolution_convert_fusion.11
  227.0 43.1 %all-gather.20.cloned.1.call-done = bf16[512,4096]{1,0:T(8,128)(2,1)} async-done(((bf16[512,1024]{1,0:T(8,128)(2,1)}), bf16[512,4096]{1,0:T(8,128)(2,1)}) %all-gather.20.cloned.1.call-update) | async-done | bytes 4194320 | tf_op jit(solution)/shard_map/all_gather | solution.py:194
  270.1 51.8 %all-gather.18.cloned.1.call-done = bf16[512,4096]{1,0:T(8,128)(2,1)} async-done(((bf16[512,128]{1,0:T(8,128)(2,1)}), bf16[512,4096]{1,0:T(8,128)(2,1)}) %all-gather.18.cloned.1.call-update) | async-done | bytes 4194320 | tf_op jit(solution)/shard_map/all_gather | solution.py:136
  321.9 5.8 convolution_convert_fusion.10
  327.9 39.7 %all-gather.14.cloned.1.call-done = bf16[16,128,896]{2,1,0:T(8,128)(2,1)} async-done(((bf16[4,128,896]{2,1,0:T(8,128)(2,1)}), bf16[16,128,896]{2,1,0:T(8,128)(2,1)}) %all-gather.14.cloned.1.call-update) | async-done | bytes 3670032 | tf_op jit(solution)/shard_map/all_gather | solution.py:169
  367.6 6.1 convolution_convert_fusion.6
  393.6 16.1 %fusion.37 = bf16[8,64,4,128]{3,1,2,0:T(8,128)(2,1)} fusion(bf16[8,256,4,128]{3,2,1,0:T(4,128)(2,1)} %reshape.289, f32[8,4,64,256]{3,2,1,0:T(8,128)} %fusion.9, f32[8,4,64,256]{3,2,1,0:T(8,128)} %get-tuple-element.48, f32[8,4,64]{2,1,0:T(4,128)S(1)} %get-tuple-element.47), kind=kOutput, calls=%fused_computation.62 | convolution fusion | flops 138152192 | bytes 6823936 | tf_op jit(solution)/shard_map/chqk,ckhd->cqhd/dot_general | solution.py:212
  411.1 6.7 convolution_convert_fusion.2
  417.9 6.7 fusion.34
  426.0 7.0 convolution_convert_fusion
  433.0 6.6 copy.112
  439.7 16.6 %convert_bitcast_fusion.1 = bf16[8,256,4,128]{1,3,2,0:T(8,128)(2,1)} fusion(f32[8,4,64,256]{3,2,1,0:T(8,128)} %fusion.9, bf16[8,64,4,128]{3,2,1,0:T(4,128)(2,1)S(1)} %reshape.288, f32[8,4,64,256]{3,2,1,0:T(8,128)} %get-tuple-element.48, f32[8,4,64]{2,1,0:T(4,128)S(1)} %get-tuple-element.47), kind=kOutput, calls=%fused_computation.29 | convolution fusion | flops 138938624 | bytes 6823936 | tf_op jit(solution)/shard_map/chqk,cqhd->ckhd/dot_general | solution.py:217
  461.1 7.0 convert_bitcast_fusion
  485.7 6.0 convolution_convert_fusion.8
  496.2 54.1 %all-to-all-done.4 = bf16[4,512,896]{2,1,0:T(8,128)(2,1)} async-done(((bf16[4,512,896]{2,1,0:T(8,128)(2,1)}), bf16[4,512,896]{2,1,0:T(8,128)(2,1)}, u32[]{:S(2)}, u32[]{:S(2)}) %all-to-all-start.4) | async-done | bytes 3670048 | tf_op jit(solution)/shard_map/all_to_all | solution.py:47
  595.9 6.6 convert_element_type.165
  602.9 48.1 %all-gather = bf16[32,4096]{1,0:T(8,128)(2,1)S(1)} all-gather(bf16[8,4096]{1,0:T(8,128)(2,1)S(1)} %convolution_convert_fusion.5), channel_id=2, replica_groups=mesh['dp'=32,'enc'=4] {'enc'}, dimensions={0}, use_global_device_ids=true | all-gather | bytes 327680 | tf_op jit(solution)/shard_map/all_gather | solution.py:12
  668.1 47.3 %reduce-scatter.6.cloned.1.call-done = bf16[128,512]{1,0:T(8,128)(2,1)} async-done(((bf16[4096,512]{1,0:T(8,128)(2,1)}), bf16[128,512]{1,0:T(8,128)(2,1)}) %reduce-scatter.6.cloned.1.call-update) | async-done | bytes 131088 | tf_op jit(solution)/shard_map/reduce_scatter | solution.py:226
  717.0 83.0 %reduce-scatter.8.cloned.1.call-done = bf16[448,128]{1,0:T(8,128)(2,1)} async-done(((bf16[14336,128]{1,0:T(8,128)(2,1)}), bf16[448,128]{1,0:T(8,128)(2,1)}) %reduce-scatter.8.cloned.1.call-update) | async-done | bytes 114704 | tf_op jit(solution)/shard_map/reduce_scatter | solution.py:57
  (157 shorter events, 157.4 us)
Async XLA Ops:
  7.2 15.1 %copy-start = (bf16[8,128,896]{2,1,0:T(8,128)(2,1)S(1)}, bf16[8,128,896]{2,1,0:T(8,128)(2,1)}, u32[]{:S(2)}) copy-start(bf16[8,128,896]{2,1,0:T(8,128)(2,1)} %param.19) | copy-start | bytes 5505028
  7.2 72.9 %all-gather.10.cloned.1.call-start = ((), (), s32[]{:S(2)}) async-start(), calls=%async_computation.9 | async-start | bytes 5242880 | tf_op jit(solution)/shard_map/all_gather | solution.py:126
  7.9 119.2 %all-gather.12.cloned.1.call-start = ((), (), s32[]{:S(2)}) async-start(), calls=%async_computation.10 | async-start | bytes 1892352 | tf_op jit(solution)/shard_map/all_gather | solution.py:133
  8.7 164.6 %all-gather.22.cloned.1.call-start = ((), (), s32[]{:S(2)}) async-start(), calls=%async_computation.18 | async-start | bytes 2162688 | tf_op jit(solution)/shard_map/all_gather | solution.py:21
  10.2 210.9 %all-gather.16.cloned.1.call-start = ((), (), s32[]{:S(2)}) async-start(), calls=%async_computation.12 | async-start | bytes 4325376 | tf_op jit(solution)/shard_map/all_gather | solution.py:131
  10.7 259.4 %all-gather.20.cloned.1.call-start = ((), (), s32[]{:S(2)}) async-start(), calls=%async_computation.14 | async-start | bytes 5242880 | tf_op jit(solution)/shard_map/all_gather | solution.py:194
  11.3 310.6 %all-gather.18.cloned.1.call-start = ((), (), s32[]{:S(2)}) async-start(), calls=%async_computation.13 | async-start | bytes 4325376 | tf_op jit(solution)/shard_map/all_gather | solution.py:136
  27.3 101.8 %all-to-all-start.1 = ((bf16[4,2,128,896]{3,2,1,0:T(8,128)(2,1)}), bf16[4,2,128,896]{3,2,1,0:T(8,128)(2,1)S(1)}, u32[]{:S(2)}, u32[]{:S(2)}) async-start(bf16[4,2,128,896]{3,2,1,0:T(8,128)(2,1)} %broadcast_select_fusion), calls=%async_computation.1 | async-start | bytes 3670016 | tf_op jit(solution)/shard_map/all_to_all | solution.py:156
  83.1 57.6 %copy-start.15 = (f32[896]{0:T(1024)S(1)}, f32[896]{0:T(1024)}, u32[]{:S(2)}) copy-start(f32[896]{0:T(1024)} %param.18) | copy-start | bytes 10756
  129.8 9.7 %all-to-all-start.2 = ((bf16[4,8,224]{2,1,0:T(8,128)(2,1)}), bf16[4,8,224]{2,1,0:T(8,128)(2,1)S(1)}, u32[]{:S(2)}, u32[]{:S(2)}) async-start(bf16[4,8,224]{2,1,0:T(8,128)(2,1)} %broadcast_in_dim.82), calls=%async_computation.2 | async-start | bytes 32768 | tf_op jit(solution)/shard_map/all_to_all | solution.py:32
  134.1 233.4 %all-gather.14.cloned.1.call-start = ((), (), s32[]{:S(2)}) async-start(), calls=%async_computation.11 | async-start | bytes 4587520 | tf_op jit(solution)/shard_map/all_gather | solution.py:169
  142.1 514.0 %all-reduce.2.cloned.1.call-start = ((), (), s32[]{:S(2)}) async-start(), calls=%async_computation.15 | async-start | bytes 8388608 | tf_op jit(solution)/shard_map/psum | solution.py:264
  177.0 44.1 %copy-start.16 = (f32[4096]{0:T(1024)S(1)}, f32[4096]{0:T(1024)}, u32[]{:S(2)}) copy-start(f32[4096]{0:T(1024)} %param.12) | copy-start | bytes 49156
  367.6 6.1 copy-start.10
  367.6 6.1 copy-start.17
  411.1 6.7 copy-start.13
  417.9 248.5 %reduce-scatter.10.cloned.1.call-start = ((), (), s32[]{:S(2)}) async-start(), calls=%async_computation.19 | async-start | bytes 4325376
  480.9 69.4 %all-to-all-start.4 = ((bf16[4,512,896]{2,1,0:T(8,128)(2,1)}), bf16[4,512,896]{2,1,0:T(8,128)(2,1)}, u32[]{:S(2)}, u32[]{:S(2)}) async-start(bf16[4,512,896]{2,1,0:T(8,128)(2,1)} %bitcast.90), calls=%async_computation.4 | async-start | bytes 7340032 | tf_op jit(solution)/shard_map/all_to_all | solution.py:47
  555.4 12.0 %all-to-all-start.5 = ((f32[4,4,896]{2,1,0:T(4,128)}), f32[4,4,896]{2,1,0:T(4,128)S(1)}, u32[]{:S(2)}, u32[]{:S(2)}) async-start(f32[4,4,896]{2,1,0:T(4,128)} %broadcast_in_dim.84), calls=%async_computation.5 | async-start | bytes 114688 | tf_op jit(solution)/shard_map/all_to_all | solution.py:32
  558.7 156.7 %reduce-scatter.6.cloned.1.call-start = ((), (), s32[]{:S(2)}) async-start(), calls=%async_computation.16 | async-start | bytes 4325376 | tf_op jit(solution)/shard_map/reduce_scatter | solution.py:226
  567.3 232.7 %reduce-scatter.8.cloned.1.call-start = ((), (), s32[]{:S(2)}) async-start(), calls=%async_computation.17 | async-start | bytes 3784704 | tf_op jit(solution)/shard_map/reduce_scatter | solution.py:57
  591.0 60.0 %all-to-all-start.3 = ((bf16[4,512,1024]{2,1,0:T(8,128)(2,1)}), bf16[4,512,1024]{2,1,0:T(8,128)(2,1)}, u32[]{:S(2)}, u32[]{:S(2)}) async-start(bf16[4,512,1024]{2,1,0:T(8,128)(2,1)} %bitcast.82), calls=%async_computation.3 | async-start | bytes 8388608 | tf_op jit(solution)/shard_map/all_to_all | solution.py:47
  595.8 6.6 copy-start.5
  662.2 141.5 %copy-start.1 = (bf16[8,128,896]{2,1,0:T(8,128)(2,1)S(1)}, bf16[8,128,896]{2,1,0:T(8,128)(2,1)}, u32[]{:S(2)}) copy-start(bf16[8,128,896]{2,1,0:T(8,128)(2,1)} %param.19) | copy-start | bytes 5505028
  (11 other events, 41.4 us)
Sparse Core Ops, SparseCore 0:
  9.7 70.3 all-gather.9
  82.3 44.7 all-gather.11
  129.9 43.2 all-gather.21
  175.4 45.6 all-gather.15
  222.6 47.5 all-gather.19
  272.2 49.7 all-gather.17
  324.2 43.3 all-gather.13
  418.0 113.4 all-reduce.1
  535.6 94.9 reduce-scatter.9
  634.1 81.2 reduce-scatter.5
  719.5 80.5 reduce-scatter.7
